TPU v7x, 32 devices: a whole 2x2x4 slice. The times are simulated.
32 devices in a mesh: grp: 2 (over x), xy: 4 (over z), guide: 4 (over y, core).
Axes of the slice: x: 2, y: 2, z: 4, core: 2. Of those that a mesh axis runs over, the one named last changes fastest.
Arguments:
- fields: float32 [2, 128, 36864], P('grp', 'guide', 'xy'), may hold values from -6 to 6
- rod_coeffs: float32 [3, 128, 4096], P(None, 'guide', 'xy'), may hold values from 0.08 to 0.32
- rod_mask: int32 [128, 4096], P('guide', 'xy'), may hold values 0 or 1
- pair_counts: int32 [4, 4], replicated, may hold values from 0 to 32, as said below
- fluid_slots: int32 [4, 4, 32], P('xy'), may hold values from 0 to 2303, as said below
- rod_slots: int32 [4, 4, 32], P('xy'), may hold values from 0 to 1023, as said below
- rod_sides: int32 [4, 4, 32], P('xy'), may hold values from 0 to 3, as said below
Outputs:
- fields_out: float32 [2, 128, 36864], P('grp', 'guide', 'xy')
Inputs may be any that keep to these rules, and one draw needn't show every extreme that they name: `pair_counts`: block [j, o] is empty where tile j + offset_o would lie past the last tile along y (o = 1, 3) or along x (o = 2, 3); block 0 of every owner holds 16 or more slots; one owner, drawn from the seed, has all its non-empty-able blocks full (32 slots). `fluid_slots`: A water column of tile t, numbered x * 48 + y, one cell out from the face of the rod in the same slot. `rod_slots`: A cell of owner j numbered rod * 16 * 16 + x * 16 + y that lies on the face of its rod named by rod_sides, also in slots past the count. `rod_sides`: 0, 1, 2, 3 name the faces x = 0, x = 15, y = 0, y = 15 of a rod, with outward normals -x, +x, -y, +y.
All inputs are finite; a program needn't handle non-finite values. No bound on the sum of `rod_mask` on one device may be relied on, other than what follows from the above.
Results may differ from a plain program's by a relative error of at most 0.00002.
Values sent between devices are 32-bit elements; how exact they have to be, the bound alone decides.
A program may use at most 64 MiB of HBM per device.

v0:
```python
import functools

import jax
import jax.numpy as jnp
from jax import lax
from jax.experimental import pallas as pl
from jax.experimental.pallas import tpu as pltpu
from jax.sharding import PartitionSpec as P

S_ROD = 16
CY = 48
STEPS = 4
TILES_Y = 4

FLUID_A = 0.55
FLUID_B = 0.5
SOFT_SHARE = 0.35

LANES = 128
HALF = 64
CHUNK = 256
MESH = pl.DeviceIdType.MESH
F32 = jnp.float32
BF16 = jnp.bfloat16


def iota(shape, dim):
    return lax.broadcasted_iota(jnp.int32, shape, dim)


def split3(values):
    hi = values.astype(BF16)
    rest = values - hi.astype(F32)
    mid = rest.astype(BF16)
    low = (rest - mid.astype(F32)).astype(BF16)
    return jnp.concatenate([hi, mid, low], axis=0)


def join3(values):
    n = values.shape[0] // 3
    return values[:n] + values[n : 2 * n] + values[2 * n :]


def dot(a, b):
    return jnp.dot(a, b, preferred_element_type=F32)


def one_hot(cond):
    return jnp.where(cond, 1.0, 0.0).astype(BF16)


def kernel(
    n_xy,
    n_guide,
    f_ref,
    c_ref,
    m_ref,
    row_ref,
    col_ref,
    o_ref,
    g_ref,
    s_ref,
    y_ref,
    mm_ref,
    lame_ref,
    shear_ref,
    be_ref,
    ebase_ref,
    send_i,
    recv_i,
    send_y,
    recv_yu,
    recv_yd,
    send_rim,
    recv_rim,
    send_x,
    recv_x,
    send_sem,
    recv_sem,
):
    levels, width = o_ref.shape
    rc = width // 9
    tc = width // 4
    rows = tc // CY
    tiles_x = n_xy // TILES_Y
    grp = lax.axis_index("grp")
    xy = lax.axis_index("xy")
    guide = lax.axis_index("guide")
    col_y = lax.rem(xy, TILES_Y)
    col_x = xy // TILES_Y
    feet = [(0, 0), (0, 1)] + ([(1, 0), (1, 1)] if tiles_x > 1 else [])
    nf = len(feet)
    up_g = lax.rem(guide + 1, n_guide)
    down_g = lax.rem(guide + n_guide - 1, n_guide)
    YU, YD, RIM, XA, XB = nf, nf + 1, nf + 2, nf + 6, nf + 7

    def foot_has(o, solid):
        dx, dy = feet[o]
        if solid:
            return jnp.logical_and(col_y + dy < TILES_Y, col_x + dx < tiles_x)
        return jnp.logical_and(col_y >= dy, col_x >= dx)

    def foot_xy(o, solid):
        dx, dy = feet[o]
        off = dx * TILES_Y + dy
        return lax.rem(xy + off, n_xy) if solid else lax.rem(xy + n_xy - off, n_xy)

    def copy(src, dst, ch, s, device):
        return pltpu.make_async_remote_copy(
            src_ref=src,
            dst_ref=dst,
            send_sem=send_sem.at[ch, s],
            recv_sem=recv_sem.at[ch, s],
            device_id=device,
            device_id_type=MESH,
        )

    def c_foot(o, s, solid):
        return copy(
            send_i.at[s],
            recv_i.at[s, o],
            o,
            s,
            {"grp": 1 - grp, "xy": foot_xy(o, solid)},
        )

    def c_up(s):
        return copy(send_y.at[s], recv_yu.at[s], YU, s, {"xy": lax.rem(xy + n_xy - 1, n_xy)})

    def c_down(s):
        return copy(send_y.at[s], recv_yd.at[s], YD, s, {"xy": lax.rem(xy + 1, n_xy)})

    def c_rim(kind, s, size):
        cols = pl.ds(0, size)
        return copy(
            send_rim.at[kind, s, :, cols],
            recv_rim.at[kind, s, :, cols],
            RIM + kind,
            s,
            {"guide": down_g if kind % 2 else up_g},
        )

    def c_x(which, s):
        off = n_xy - TILES_Y if which == 0 else TILES_Y
        return copy(
            send_x.at[which, s],
            recv_x.at[which, s],
            XA + which,
            s,
            {"xy": lax.rem(xy + off, n_xy)},
        )

    has_next_y = col_y < TILES_Y - 1
    has_prev_y = col_y > 0
    has_next_x = col_x < tiles_x - 1
    has_prev_x = col_x > 0

    barrier = pltpu.get_barrier_semaphore()

    def greet(device):
        pl.semaphore_signal(barrier, inc=1, device_id=device, device_id_type=MESH)

    greet({"guide": up_g})
    greet({"guide": down_g})
    for solid in (True, False):
        for o in range(nf):
            mine = (grp == 0) if solid else (grp != 0)

            @pl.when(jnp.logical_and(mine, foot_has(o, solid)))
            def _():
                greet({"grp": 1 - grp, "xy": foot_xy(o, solid)})

    sides = [(has_next_y, 1), (has_prev_y, n_xy - 1)]
    if tiles_x > 1:
        sides += [(has_next_x, TILES_Y), (has_prev_x, n_xy - TILES_Y)]
    for has, off in sides:

        @pl.when(jnp.logical_and(grp != 0, has))
        def _():
            greet({"xy": lax.rem(xy + off, n_xy)})

    def as_int(cond):
        return jnp.where(cond, 1, 0)

    solid_n = sum(as_int(foot_has(o, True)) for o in range(nf))
    fluid_n = sum(as_int(foot_has(o, False)) for o in range(nf)) + sum(as_int(h) for h, _ in sides)
    expect = 2 + jnp.where(grp == 0, solid_n, fluid_n)

    row_idx = row_ref[0:1, :]
    facing = row_ref[1:2, :].astype(F32)
    lane = iota((levels, LANES), 1)
    level8 = iota((8, 1), 0)
    slots = LANES // 4

    def comp(ref, member, size, r0):
        return ref[r0 : r0 + 8, member * size : (member + 1) * size]

    def lower(member, size, r0, rim):
        if r0 == 0:
            block = comp(o_ref, member, size, 0)
            return jnp.where(level8 == 0, rim, pltpu.roll(block, 1, 0))
        return o_ref[r0 - 1 : r0 + 7, member * size : (member + 1) * size]

    def upper(member, size, r0, rim):
        if r0 == levels - 8:
            block = comp(o_ref, member, size, r0)
            return jnp.where(level8 == 7, rim, pltpu.roll(block, 7, 0))
        return o_ref[r0 + 1 : r0 + 9, member * size : (member + 1) * size]

    def gather(start, size, lanes):
        acc = None
        for c in range(0, size, CHUNK):
            part = dot(
                split3(o_ref[:, start + c : start + c + CHUNK]),
                g_ref[c : c + CHUNK, lanes[0] : lanes[1]],
            )
            acc = part if acc is None else acc + part
        return join3(acc)

    def incoming(s):
        arrived = recv_i[s, 0]
        for o in range(1, nf):
            arrived = jnp.where(lane >= o * slots, recv_i[s, o], arrived)
        return jnp.where(lane < nf * slots, arrived, 0.0)

    def each_foot(solid, act):
        for o in range(nf):

            @pl.when(foot_has(o, solid))
            def _():
                act(o)

    def no_feet(solid):
        for o in range(1, nf):

            @pl.when(jnp.logical_not(foot_has(o, solid)))
            def _():
                recv_i[:, o] = jnp.zeros((STEPS, levels, LANES), F32)

    @pl.when(grp == 0)
    def _():
        o_ref[...] = f_ref[...]
        no_feet(True)

        def put_a(s):
            top = levels - 1
            send_rim[0, s, :, 0 : 2 * rc] = o_ref[top : top + 1, 7 * rc : 9 * rc]
            send_rim[1, s, :, 0:rc] = o_ref[0:1, 5 * rc : 6 * rc]
            c_rim(0, s, 2 * rc).start()
            c_rim(1, s, rc).start()

        pl.semaphore_wait(barrier, expect)
        put_a(0)
        for c in range(0, 2 * rc, CHUNK):
            g_ref[c : c + CHUNK, 0:LANES] = one_hot(iota((CHUNK, LANES), 0) + c == row_idx)
            s_ref[0:LANES, c : c + CHUNK] = one_hot(iota((LANES, CHUNK), 1) + c == col_ref[...])
        mm_ref[0:LANES, 0:LANES] = one_hot(col_ref[...] == row_idx)
        for r0 in range(0, levels, 8):
            soft = jnp.where(m_ref[r0 : r0 + 8, :] == 1, 1.0, SOFT_SHARE).astype(F32)
            lame_ref[r0 : r0 + 8, :] = c_ref[0, r0 : r0 + 8, :] * soft
            shear_ref[r0 : r0 + 8, :] = c_ref[1, r0 : r0 + 8, :] * soft
        acc = None
        for c in range(0, 2 * rc, CHUNK):
            part = dot(
                split3(c_ref[2, :, c % rc : c % rc + CHUNK]), g_ref[c : c + CHUNK, 0:LANES]
            )
            acc = part if acc is None else acc + part
        be_ref[...] = join3(acc)

        place = iota((1, rc), 1)
        in_x = place // S_ROD % S_ROD
        in_y = place % S_ROD

        def fore_x(v):
            return jnp.where(in_x < S_ROD - 1, pltpu.roll(v, rc - S_ROD, 1), 0.0) - v

        def back_x(v):
            return v - jnp.where(in_x > 0, pltpu.roll(v, S_ROD, 1), 0.0)

        def fore_y(v):
            return jnp.where(in_y < S_ROD - 1, pltpu.roll(v, rc - 1, 1), 0.0) - v

        def back_y(v):
            return v - jnp.where(in_y > 0, pltpu.roll(v, 1, 1), 0.0)

        def store(member, r0, v):
            o_ref[r0 : r0 + 8, member * rc : (member + 1) * rc] = v

        def step(s, carry):
            c_rim(0, s, 2 * rc).wait_recv()
            c_rim(1, s, rc).wait_recv()
            for r0 in range(0, levels, 8):
                buo = c_ref[2, r0 : r0 + 8, :]
                xy_ = comp(o_ref, 6, rc, r0)
                xz = comp(o_ref, 7, rc, r0)
                yz = comp(o_ref, 8, rc, r0)
                xz_lo = lower(7, rc, r0, recv_rim[0, s, :, 0:rc])
                yz_lo = lower(8, rc, r0, recv_rim[0, s, :, rc : 2 * rc])
                store(
                    0,
                    r0,
                    comp(o_ref, 0, rc, r0)
                    + buo * (fore_x(comp(o_ref, 3, rc, r0)) + back_y(xy_) + (xz - xz_lo)),
                )
                store(
                    1,
                    r0,
                    comp(o_ref, 1, rc, r0)
                    + buo * (back_x(xy_) + fore_y(comp(o_ref, 4, rc, r0)) + (yz - yz_lo)),
                )
                zz = comp(o_ref, 5, rc, r0)
                zz_up = upper(5, rc, r0, recv_rim[1, s, :, 0:rc])
                store(
                    2,
                    r0,
                    comp(o_ref, 2, rc, r0) + buo * (back_x(xz) + back_y(yz) + (zz_up - zz)),
                )
            send_rim[2, s, :, 0:rc] = o_ref[levels - 1 : levels, 2 * rc : 3 * rc]
            c_rim(2, s, rc).start()
            base = gather(0, 2 * rc, (0, LANES))
            each_foot(True, lambda o: c_foot(o, s, True).wait_recv())
            lhs = split3(incoming(s) * (-facing))
            normal = base + be_ref[...] * join3(dot(lhs, mm_ref[0:LANES, 0:LANES]))
            send_i[s] = normal * facing
            each_foot(True, lambda o: c_foot(o, s, True).start())
            for c in range(0, 2 * rc, CHUNK):
                push = join3(dot(lhs, s_ref[0:LANES, c : c + CHUNK]))
                o_ref[:, c : c + CHUNK] += c_ref[2, :, c % rc : c % rc + CHUNK] * push
            send_rim[3, s, :, 0 : 2 * rc] = o_ref[0:1, 0 : 2 * rc]
            c_rim(3, s, 2 * rc).start()
            c_rim(2, s, rc).wait_recv()
            c_rim(3, s, 2 * rc).wait_recv()
            for r0 in range(0, levels, 8):
                sx = comp(o_ref, 0, rc, r0)
                sy = comp(o_ref, 1, rc, r0)
                sz = comp(o_ref, 2, rc, r0)
                lame = lame_ref[r0 : r0 + 8, :]
                shear = shear_ref[r0 : r0 + 8, :]
                spread_x = back_x(sx)
                spread_y = back_y(sy)
                spread_z = sz - lower(2, rc, r0, recv_rim[2, s, :, 0:rc])
                bulk = lame * (spread_x + spread_y + spread_z)
                twice = 2.0 * shear
                store(3, r0, comp(o_ref, 3, rc, r0) + bulk + twice * spread_x)
                store(4, r0, comp(o_ref, 4, rc, r0) + bulk + twice * spread_y)
                store(5, r0, comp(o_ref, 5, rc, r0) + bulk + twice * spread_z)
                store(6, r0, comp(o_ref, 6, rc, r0) + shear * (fore_y(sx) + fore_x(sy)))
                sx_up = upper(0, rc, r0, recv_rim[3, s, :, 0:rc])
                sy_up = upper(1, rc, r0, recv_rim[3, s, :, rc : 2 * rc])
                store(7, r0, comp(o_ref, 7, rc, r0) + shear * (sx_up - sx + fore_x(sz)))
                store(8, r0, comp(o_ref, 8, rc, r0) + shear * (sy_up - sy + fore_y(sz)))

            @pl.when(s < STEPS - 1)
            def _():
                put_a(s + 1)

            return carry

        lax.fori_loop(0, STEPS, step, 0)

        def drain(s, carry):
            for kind, size in ((0, 2 * rc), (1, rc), (2, rc), (3, 2 * rc)):
                c_rim(kind, s, size).wait_send()
            each_foot(True, lambda o: c_foot(o, s, True).wait_send())
            return carry

        lax.fori_loop(0, STEPS, drain, 0)

    @pl.when(grp != 0)
    def _():
        o_ref[...] = f_ref[...]
        no_feet(False)

        @pl.when(jnp.logical_not(has_next_y))
        def _():
            recv_yu[...] = jnp.zeros_like(recv_yu)

        @pl.when(jnp.logical_not(has_prev_y))
        def _():
            recv_yd[...] = jnp.zeros_like(recv_yd)

        if tiles_x > 1:

            @pl.when(jnp.logical_not(has_next_x))
            def _():
                recv_x[0] = jnp.zeros((STEPS, levels, LANES), F32)

            @pl.when(jnp.logical_not(has_prev_x))
            def _():
                recv_x[1] = jnp.zeros((STEPS, levels, LANES), F32)

        pl.semaphore_wait(barrier, expect)
        edge = iota((1, LANES), 1)
        edge_cols = jnp.where(
            edge < rows,
            edge * CY,
            jnp.where(
                jnp.logical_and(edge >= HALF, edge < HALF + rows),
                (edge - HALF) * CY + CY - 1,
                -2,
            ),
        )
        spot = iota((LANES, 1), 0)
        first_spots = jnp.where(spot < rows, spot * CY, -1)
        last_spots = jnp.where(spot < rows, spot * CY + CY - 1, -1)

        def put_rim(s):
            send_rim[1, s, :, 0:tc] = o_ref[0:1, 0:tc]
            c_rim(1, s, tc).start()
            if tiles_x > 1:
                send_x[0, s] = o_ref[:, 0:LANES]

                @pl.when(has_prev_x)
                def _():
                    c_x(0, s).start()

        def put_samples(s, samples):
            send_i[s] = samples[:, :LANES]
            send_y[s] = samples[:, LANES:]
            each_foot(False, lambda o: c_foot(o, s, False).start())

            @pl.when(has_prev_y)
            def _():
                c_up(s).start()

            @pl.when(has_next_y)
            def _():
                c_down(s).start()

        put_rim(0)
        for c in range(0, tc, CHUNK):
            g_ref[c : c + CHUNK, 0:LANES] = one_hot(iota((CHUNK, LANES), 0) + c == row_idx)
            g_ref[c : c + CHUNK, LANES:] = one_hot(iota((CHUNK, LANES), 0) + c == edge_cols)
        put_samples(0, gather(0, tc, (0, 2 * LANES)))
        send_y[STEPS] = gather(2 * tc, tc, (LANES, 2 * LANES))

        @pl.when(has_next_y)
        def _():
            c_down(STEPS).start()

        for c in range(0, tc, CHUNK):
            at = iota((LANES, CHUNK), 1) + c
            s_ref[0:LANES, c : c + CHUNK] = one_hot(at == col_ref[...])
            s_ref[LANES:, c : c + CHUNK] = one_hot(at == first_spots)
            y_ref[:, c : c + CHUNK] = one_hot(at == last_spots)
        mm_ref[0:LANES, 0:LANES] = one_hot(col_ref[...] == row_idx)
        mm_ref[0:LANES, LANES:] = one_hot(col_ref[...] == edge_cols)
        mm_ref[LANES:, 0:LANES] = one_hot(first_spots == row_idx)
        mm_ref[LANES:, LANES:] = one_hot(first_spots == edge_cols)

        @pl.when(has_prev_y)
        def _():
            c_down(STEPS).wait_recv()

        be_ref[...] = jnp.where(lane < rows, pltpu.roll(recv_yd[STEPS], HALF, 1), 0.0)

        place = iota((1, tc), 1)
        in_y = place % CY

        def store(member, r0, v):
            o_ref[r0 : r0 + 8, member * tc : (member + 1) * tc] = v

        def step(s, carry):
            c_rim(1, s, tc).wait_recv()
            if tiles_x > 1:

                @pl.when(has_next_x)
                def _():
                    c_x(0, s).wait_recv()

            for r0 in range(0, levels, 8):
                p = comp(o_ref, 0, tc, r0)
                next_x = jnp.where(place < tc - CY, pltpu.roll(p, tc - CY, 1), 0.0)
                store(1, r0, comp(o_ref, 1, tc, r0) - FLUID_B * (next_x - p))
                next_y = jnp.where(in_y < CY - 1, pltpu.roll(p, tc - 1, 1), 0.0)
                store(2, r0, comp(o_ref, 2, tc, r0) - FLUID_B * (next_y - p))
                next_z = upper(0, tc, r0, recv_rim[1, s, :, 0:tc])
                store(3, r0, comp(o_ref, 3, tc, r0) - FLUID_B * (next_z - p))
            send_rim[2, s, :, 0:tc] = o_ref[levels - 1 : levels, 3 * tc : 4 * tc]
            c_rim(2, s, tc).start()
            if tiles_x > 1:
                ahead = pltpu.roll(recv_x[0, s], LANES - CY, 1)
                tail = slice(2 * tc - LANES, 2 * tc)
                o_ref[:, tail] -= jnp.where(lane >= LANES - CY, FLUID_B * ahead, 0.0)
                send_x[1, s] = o_ref[:, tail]

                @pl.when(has_next_x)
                def _():
                    c_x(1, s).start()

            @pl.when(has_next_y)
            def _():
                c_up(s).wait_recv()

            @pl.when(has_prev_y)
            def _():
                c_down(s).wait_recv()

            lhs = split3(recv_yu[s])
            for c in range(0, tc, CHUNK):
                o_ref[:, 2 * tc + c : 2 * tc + c + CHUNK] -= FLUID_B * join3(
                    dot(lhs, y_ref[:, c : c + CHUNK])
                )
            behind = be_ref[...] - FLUID_B * (send_y[s] - pltpu.roll(recv_yd[s], HALF, 1))
            behind = jnp.where(jnp.logical_and(lane < rows, has_prev_y), behind, 0.0)
            be_ref[...] = behind

            c_rim(2, s, tc).wait_recv()
            for r0 in range(0, levels, 8):
                fx = comp(o_ref, 1, tc, r0)
                fy = comp(o_ref, 2, tc, r0)
                fz = comp(o_ref, 3, tc, r0)
                prev_x = jnp.where(place >= CY, pltpu.roll(fx, CY, 1), 0.0)
                prev_y = jnp.where(in_y > 0, pltpu.roll(fy, 1, 1), 0.0)
                prev_z = lower(3, tc, r0, recv_rim[2, s, :, 0:tc])
                store(
                    0,
                    r0,
                    comp(o_ref, 0, tc, r0)
                    - FLUID_A * ((fx - prev_x) + (fy - prev_y) + (fz - prev_z)),
                )
            if tiles_x > 1:

                @pl.when(has_prev_x)
                def _():
                    c_x(1, s).wait_recv()

                before = pltpu.roll(recv_x[1, s], CY, 1)
                o_ref[:, 0:LANES] += jnp.where(lane < CY, FLUID_A * before, 0.0)

            @pl.when(s < STEPS - 1)
            def _():
                ebase_ref[...] = gather(0, tc, (0, 2 * LANES))

            each_foot(False, lambda o: c_foot(o, s, False).wait_recv())
            lhs = split3(jnp.concatenate([incoming(s), behind], axis=1))

            @pl.when(s < STEPS - 1)
            def _():
                put_samples(
                    s + 1, ebase_ref[...] + FLUID_A * join3(dot(lhs, mm_ref[...]))
                )

            for c in range(0, tc, CHUNK):
                o_ref[:, c : c + CHUNK] += FLUID_A * join3(dot(lhs, s_ref[:, c : c + CHUNK]))

            @pl.when(s < STEPS - 1)
            def _():
                put_rim(s + 1)

            return carry

        lax.fori_loop(0, STEPS, step, 0)

        def drain(s, carry):
            c_rim(1, s, tc).wait_send()
            c_rim(2, s, tc).wait_send()
            each_foot(False, lambda o: c_foot(o, s, False).wait_send())

            @pl.when(has_prev_y)
            def _():
                c_up(s).wait_send()

            @pl.when(has_next_y)
            def _():
                c_down(s).wait_send()

            if tiles_x > 1:

                @pl.when(has_prev_x)
                def _():
                    c_x(0, s).wait_send()

                @pl.when(has_next_x)
                def _():
                    c_x(1, s).wait_send()

            return carry

        lax.fori_loop(0, STEPS, drain, 0)

        @pl.when(has_next_y)
        def _():
            c_down(STEPS).wait_send()


def local(n_xy, n_guide, fields, rod_coeffs, rod_mask, pair_counts, fluid_slots, rod_slots, rod_sides):
    levels, width = fields.shape[1:]
    rc, tc = width // 9, width // 4
    tile = lax.axis_index("xy")
    is_solid = lax.axis_index("grp") == 0
    slots = fluid_slots.shape[2]
    offsets = jnp.array([0, 1, TILES_Y, TILES_Y + 1], dtype=jnp.int32)
    owner_ids = jnp.arange(n_xy, dtype=jnp.int32)[:, None]
    owners = jnp.where(is_solid, tile, (tile - offsets) % n_xy)
    counts = jnp.sum(jnp.where(owner_ids == owners[None, :], pair_counts, 0), axis=0)
    valid = (jnp.arange(slots, dtype=jnp.int32)[None, :] < counts[:, None]).reshape(-1)
    sides = rod_sides[0].reshape(-1)
    cols = jnp.where(
        is_solid, sides // 2 * rc + rod_slots[0].reshape(-1), fluid_slots[0].reshape(-1)
    )
    facing = 2 * (sides % 2) - 1
    row = jnp.stack([cols, facing])
    col = jnp.where(valid, cols, -1).reshape(-1, 1)
    n_feet = 4 if n_xy > TILES_Y else 2
    n_x = 2 if n_xy > TILES_Y else 1
    x_steps = STEPS if n_xy > TILES_Y else 1
    rim = max(2 * rc, tc)
    vmem = pl.BlockSpec(memory_space=pltpu.VMEM)
    out = pl.pallas_call(
        functools.partial(kernel, n_xy, n_guide),
        out_shape=jax.ShapeDtypeStruct((levels, width), F32),
        in_specs=[vmem] * 5,
        out_specs=vmem,
        scratch_shapes=[
            pltpu.VMEM((tc, 2 * LANES), BF16),
            pltpu.VMEM((2 * LANES, tc), BF16),
            pltpu.VMEM((LANES, tc), BF16),
            pltpu.VMEM((2 * LANES, 2 * LANES), BF16),
            pltpu.VMEM((levels, rc), F32),
            pltpu.VMEM((levels, rc), F32),
            pltpu.VMEM((levels, LANES), F32),
            pltpu.VMEM((levels, 2 * LANES), F32),
            pltpu.VMEM((STEPS, levels, LANES), F32),
            pltpu.VMEM((STEPS, n_feet, levels, LANES), F32),
            pltpu.VMEM((STEPS + 1, levels, LANES), F32),
            pltpu.VMEM((STEPS + 1, levels, LANES), F32),
            pltpu.VMEM((STEPS + 1, levels, LANES), F32),
            pltpu.VMEM((4, STEPS, 1, rim), F32),
            pltpu.VMEM((4, STEPS, 1, rim), F32),
            pltpu.VMEM((n_x, x_steps, levels, LANES), F32),
            pltpu.VMEM((n_x, x_steps, levels, LANES), F32),
            pltpu.SemaphoreType.DMA((n_feet + 8, STEPS + 1)),
            pltpu.SemaphoreType.DMA((n_feet + 8, STEPS + 1)),
        ],
        compiler_params=pltpu.CompilerParams(collective_id=0, has_side_effects=True),
    )(fields[0], rod_coeffs, rod_mask, row, col)
    return out[None]


def solution(mesh):
    return jax.shard_map(
        functools.partial(local, mesh.shape["xy"], mesh.shape["guide"]),
        mesh=mesh,
        in_specs=(
            P("grp", "guide", "xy"),
            P(None, "guide", "xy"),
            P("guide", "xy"),
            P(),
            P("xy", None, None),
            P("xy", None, None),
            P("xy", None, None),
        ),
        out_specs=P("grp", "guide", "xy"),
        check_vma=False,
    )
```

profile of v0, /device:TPU:1, one launch (start us, length us, event | category | flops | bytes accessed | tf_op | source)
XLA Modules:
  0.0 44.6 jit_solution(119107495357311869)
XLA Ops:
  0.0 0.7 %broadcast_select_fusion = s32[4]{0:T(128)S(1)} fusion(pred[]{:T(512)S(6)} %eq.20, s32[4]{0:T(128)} %constant.65, s32[]{:T(128)S(6)} %axis_index.28), kind=kLoop, calls=%fused_computation.23 | loop fusion | flops 52 | bytes 37 | tf_op jit(solution)/shard_map/jit(_where)/select_n | solution.py:595
  0.7 0.7 %select_reduce_fusion = s32[4]{0:T(128)S(1)} fusion(s32[4,4]{1,0:T(4,128)} %param.11, s32[4]{0:T(128)S(1)} %broadcast_select_fusion), kind=kLoop, calls=%fused_computation.13 | loop fusion | flops 44 | bytes 96 | tf_op jit(solution)/shard_map/reduce_sum | solution.py:596
  1.4 0.1 iota_compare_fusion.1
  1.4 0.8 %reshape_squeeze.17 = s32[1,128]{1,0:T(1,128)S(1)} reshape(s32[1,4,32]{2,1,0:T(4,128)} %param.12) | data formatting | bytes 1024 | tf_op jit(solution)/shard_map/reshape;squeeze | solution.py:600
  2.2 0.8 %reshape_squeeze.16 = s32[1,128]{1,0:T(1,128)S(1)} reshape(s32[1,4,32]{2,1,0:T(4,128)} %param.13) | data formatting | bytes 1024 | tf_op jit(solution)/shard_map/reshape;squeeze | solution.py:600
  3.0 0.8 %reshape_squeeze.15 = s32[1,128]{1,0:T(1,128)S(1)} reshape(s32[1,4,32]{2,1,0:T(4,128)} %param.14) | data formatting | bytes 1024 | tf_op jit(solution)/shard_map/reshape;squeeze | solution.py:598
  3.7 0.6 %pad_add_fusion.row_ref = s32[2,128]{1,0:T(2,128)} fusion(s32[1,128]{1,0:T(1,128)S(1)} %get-tuple-element.6, s32[1,128]{1,0:T(1,128)S(1)} %get-tuple-element.5), kind=kLoop, calls=%fused_computation.22 | loop fusion | flops 256 | bytes 2048 | tf_op jit(solution)/shard_map/stack | solution.py:603
  4.3 0.1 lt.42
  4.5 0.8 %reshape_squeeze.23 = s32[128,1]{1,0:T(8,128)S(1)} reshape(s32[1,4,32]{2,1,0:T(4,128)} %param.12) | data formatting | bytes 1024 | tf_op jit(solution)/shard_map/reshape;squeeze | solution.py:600
  5.3 0.8 %reshape_squeeze.22 = s32[128,1]{1,0:T(8,128)S(1)} reshape(s32[1,4,32]{2,1,0:T(4,128)} %param.13) | data formatting | bytes 1024 | tf_op jit(solution)/shard_map/reshape;squeeze | solution.py:600
  6.0 0.8 %reshape_squeeze.21 = s32[128,1]{1,0:T(8,128)S(1)} reshape(s32[1,4,32]{2,1,0:T(4,128)} %param.14) | data formatting | bytes 1024 | tf_op jit(solution)/shard_map/reshape;squeeze | solution.py:598
  6.8 0.7 %fusion.4.col_ref = s32[128,1]{1,0:T(8,128)} fusion(pred[128,1]{1,0:T(8,128)(4,1)S(1)} %lt.42, s32[128,1]{1,0:T(8,128)S(1)} %reshape_squeeze.23, s32[128,1]{1,0:T(8,128)S(1)} %reshape_squeeze.22, s32[128,1]{1,0:T(8,128)S(1)} %reshape_squeeze.21, pred[]{:T(512)S(6)} %eq.20), kind=kLoop, calls=%fused_computation.8 | loop fusion | flops 2432 | bytes 2177 | tf_op jit(solution)/shard_map/jit(_where)/select_n | solution.py:604
  7.5 34.7 %shard_map.82 = f32[32,9216]{1,0:T(8,128)} custom-call(f32[32,9216]{1,0:T(8,128)} %bitcast.3, f32[3,32,1024]{2,1,0:T(8,128)} %c_ref.1, s32[32,1024]{1,0:T(8,128)} %m_ref.1, s32[2,128]{1,0:T(2,128)} %pad_add_fusion.row_ref, s32[128,1]{1,0:T(8,128)} %fusion.4.col_ref), custom_call_target="tpu_custom_call" | custom-call | tf_op jit(solution)/shard_map/pallas_call | solution.py:610
  42.3 2.4 %copy.17 = f32[1,32,9216]{2,1,0:T(8,128)} copy(f32[1,32,9216]{2,1,0:T(8,128)} %bitcast.2) | data formatting | bytes 2359296
  (1 shorter events, 0.0 us)
where the time goes:
time: 45 us; the launch traced here: 44.6 us
  Pallas kernels  34.7 us (77%)
  local copies, waits for them, and re-layouts  7.13 us (16%)
  other arithmetic  2.72 us (6%)
    pallas_call x1, Pallas kernels, local(): pl.pallas_call(functools.partial(kernel, n_xy, n_guide), out_shape=jax.Sh...  34.7 us
    unnamed x1, local copies, waits for them, and re-layouts  2.36 us
    another operation x2, local copies, waits for them, and re-layouts, local(): rod_slots[0].reshape(-1)  1.55 us
    another operation x2, local copies, waits for them, and re-layouts, local(): sides = rod_sides[0].reshape(-1)  1.55 us
    another operation x2, local copies, waits for them, and re-layouts, local(): fluid_slots[0].reshape(-1)  1.55 us

commit v1 on v0

--- a/solution.py
+++ b/solution.py
@@ -52,12 +52,17 @@
 def kernel(
     n_xy,
     n_guide,
-    f_ref,
+    f_hbm,
+    c_hbm,
+    m_hbm,
+    counts_ref,
+    fluid_ref,
+    rod_ref,
+    sides_ref,
+    o_ref,
     c_ref,
     m_ref,
-    row_ref,
-    col_ref,
-    o_ref,
+    in_sem,
     g_ref,
     s_ref,
     y_ref,
@@ -68,6 +73,7 @@
     ebase_ref,
     send_i,
     recv_i,
+    own_y,
     send_y,
     recv_yu,
     recv_yd,
@@ -92,6 +98,19 @@
     nf = len(feet)
     up_g = lax.rem(guide + 1, n_guide)
     down_g = lax.rem(guide + n_guide - 1, n_guide)
+    slots = fluid_ref.shape[2]
+    bands = levels // 8
+    half = levels // 2
+    load_f = pltpu.make_async_copy(f_hbm, o_ref, in_sem.at[0])
+    load_c = pltpu.make_async_copy(c_hbm, c_ref, in_sem.at[1])
+    load_m = pltpu.make_async_copy(m_hbm, m_ref, in_sem.at[2])
+    load_f.start()
+
+    @pl.when(grp == 0)
+    def _():
+        load_c.start()
+        load_m.start()
+
     YU, YD, RIM, XA, XB = nf, nf + 1, nf + 2, nf + 6, nf + 7
 
     def foot_has(o, solid):
@@ -117,7 +136,7 @@
 
     def c_foot(o, s, solid):
         return copy(
-            send_i.at[s],
+            send_i.at[s, o],
             recv_i.at[s, o],
             o,
             s,
@@ -125,10 +144,10 @@
         )
 
     def c_up(s):
-        return copy(send_y.at[s], recv_yu.at[s], YU, s, {"xy": lax.rem(xy + n_xy - 1, n_xy)})
+        return copy(send_y.at[0, s], recv_yu.at[s], YU, s, {"xy": lax.rem(xy + n_xy - 1, n_xy)})
 
     def c_down(s):
-        return copy(send_y.at[s], recv_yd.at[s], YD, s, {"xy": lax.rem(xy + 1, n_xy)})
+        return copy(send_y.at[1, s], recv_yd.at[s], YD, s, {"xy": lax.rem(xy + 1, n_xy)})
 
     def c_rim(kind, s, size):
         cols = pl.ds(0, size)
@@ -186,11 +205,43 @@
     fluid_n = sum(as_int(foot_has(o, False)) for o in range(nf)) + sum(as_int(h) for h, _ in sides)
     expect = 2 + jnp.where(grp == 0, solid_n, fluid_n)
 
-    row_idx = row_ref[0:1, :]
-    facing = row_ref[1:2, :].astype(F32)
     lane = iota((levels, LANES), 1)
+    lane8 = iota((8, LANES), 1)
     level8 = iota((8, 1), 0)
-    slots = LANES // 4
+    spot = iota((LANES, 1), 0)
+    pick = iota((LANES, slots), 1) == iota((LANES, slots), 0) % slots
+    diagonal = iota((LANES, LANES), 0) == iota((LANES, LANES), 1)
+
+    def as_column(table):
+        wide = jnp.concatenate(
+            [jnp.broadcast_to(table[o : o + 1, :], (slots, slots)) for o in range(LANES // slots)],
+            axis=0,
+        )
+        return jnp.sum(jnp.where(pick, wide.astype(F32), 0.0), axis=1, keepdims=True)
+
+    def as_row(column):
+        return jnp.sum(jnp.where(diagonal, column, 0.0), axis=0, keepdims=True)
+
+    def slot_columns(table, owner_of):
+        column = as_column(table)
+        row = as_row(column).astype(jnp.int32)
+        column = column.astype(jnp.int32)
+        count = jnp.zeros((LANES, 1), jnp.int32)
+        for o in range(nf):
+            count = jnp.where(spot // slots == o, counts_ref[owner_of(o), o], count)
+        return row, jnp.where(spot % slots < count, column, -1)
+
+    def pack(samples, o):
+        out = pltpu.roll(samples[0:8], (-o * slots) % LANES, 1)
+        for b in range(1, bands):
+            moved = pltpu.roll(samples[8 * b : 8 * b + 8], ((b - o) * slots) % LANES, 1)
+            out = jnp.where(lane8 >= b * slots, moved, out)
+        return out
+
+    def unfold(packed):
+        return jnp.concatenate([packed, pltpu.roll(packed, HALF, 1)], axis=0)
+
+    left = iota((half, LANES), 1) < HALF
 
     def comp(ref, member, size, r0):
         return ref[r0 : r0 + 8, member * size : (member + 1) * size]
@@ -218,10 +269,14 @@
         return join3(acc)
 
     def incoming(s):
-        arrived = recv_i[s, 0]
-        for o in range(1, nf):
-            arrived = jnp.where(lane >= o * slots, recv_i[s, o], arrived)
-        return jnp.where(lane < nf * slots, arrived, 0.0)
+        blocks = []
+        for b in range(bands):
+            block = pltpu.roll(recv_i[s, 0], (-b * slots) % LANES, 1)
+            for o in range(1, nf):
+                moved = pltpu.roll(recv_i[s, o], ((o - b) * slots) % LANES, 1)
+                block = jnp.where(lane8 >= o * slots, moved, block)
+            blocks.append(block)
+        return jnp.where(lane < nf * slots, jnp.concatenate(blocks, axis=0), 0.0)
 
     def each_foot(solid, act):
         for o in range(nf):
@@ -235,12 +290,19 @@
 
             @pl.when(jnp.logical_not(foot_has(o, solid)))
             def _():
-                recv_i[:, o] = jnp.zeros((STEPS, levels, LANES), F32)
+                recv_i[:, o] = jnp.zeros((STEPS, 8, LANES), F32)
 
     @pl.when(grp == 0)
     def _():
-        o_ref[...] = f_ref[...]
         no_feet(True)
+        sides = sides_ref[0]
+        row_idx, col_idx = slot_columns(sides // 2 * rc + rod_ref[0], lambda o: xy)
+        facing = 2.0 * as_row(as_column(sides % 2)) - 1.0
+        for c in range(0, 2 * rc, CHUNK):
+            g_ref[c : c + CHUNK, 0:LANES] = one_hot(iota((CHUNK, LANES), 0) + c == row_idx)
+            s_ref[0:LANES, c : c + CHUNK] = one_hot(iota((LANES, CHUNK), 1) + c == col_idx)
+        mm_ref[0:LANES, 0:LANES] = one_hot(col_idx == row_idx)
+        load_f.wait()
 
         def put_a(s):
             top = levels - 1
@@ -251,10 +313,8 @@
 
         pl.semaphore_wait(barrier, expect)
         put_a(0)
-        for c in range(0, 2 * rc, CHUNK):
-            g_ref[c : c + CHUNK, 0:LANES] = one_hot(iota((CHUNK, LANES), 0) + c == row_idx)
-            s_ref[0:LANES, c : c + CHUNK] = one_hot(iota((LANES, CHUNK), 1) + c == col_ref[...])
-        mm_ref[0:LANES, 0:LANES] = one_hot(col_ref[...] == row_idx)
+        load_c.wait()
+        load_m.wait()
         for r0 in range(0, levels, 8):
             soft = jnp.where(m_ref[r0 : r0 + 8, :] == 1, 1.0, SOFT_SHARE).astype(F32)
             lame_ref[r0 : r0 + 8, :] = c_ref[0, r0 : r0 + 8, :] * soft
@@ -321,7 +381,9 @@
             each_foot(True, lambda o: c_foot(o, s, True).wait_recv())
             lhs = split3(incoming(s) * (-facing))
             normal = base + be_ref[...] * join3(dot(lhs, mm_ref[0:LANES, 0:LANES]))
-            send_i[s] = normal * facing
+            normal = normal * facing
+            for o in range(nf):
+                send_i[s, o] = pack(normal, o)
             each_foot(True, lambda o: c_foot(o, s, True).start())
             for c in range(0, 2 * rc, CHUNK):
                 push = join3(dot(lhs, s_ref[0:LANES, c : c + CHUNK]))
@@ -368,7 +430,6 @@
 
     @pl.when(grp != 0)
     def _():
-        o_ref[...] = f_ref[...]
         no_feet(False)
 
         @pl.when(jnp.logical_not(has_next_y))
@@ -389,7 +450,7 @@
             def _():
                 recv_x[1] = jnp.zeros((STEPS, levels, LANES), F32)
 
-        pl.semaphore_wait(barrier, expect)
+        row_idx, col_idx = slot_columns(fluid_ref[0], lambda o: foot_xy(o, False))
         edge = iota((1, LANES), 1)
         edge_cols = jnp.where(
             edge < rows,
@@ -400,7 +461,6 @@
                 -2,
             ),
         )
-        spot = iota((LANES, 1), 0)
         first_spots = jnp.where(spot < rows, spot * CY, -1)
         last_spots = jnp.where(spot < rows, spot * CY + CY - 1, -1)
 
@@ -414,10 +474,15 @@
                 def _():
                     c_x(0, s).start()
 
-        def put_samples(s, samples):
-            send_i[s] = samples[:, :LANES]
-            send_y[s] = samples[:, LANES:]
+        def put_samples(s, both):
+            samples = both[:, :LANES]
+            for o in range(nf):
+                send_i[s, o] = pack(samples, o)
             each_foot(False, lambda o: c_foot(o, s, False).start())
+            edges = both[:, LANES:]
+            own_y[...] = edges
+            send_y[0, s] = jnp.where(left, edges[:half], pltpu.roll(edges[half:], HALF, 1))
+            send_y[1, s] = jnp.where(left, pltpu.roll(edges[:half], HALF, 1), edges[half:])
 
             @pl.when(has_prev_y)
             def _():
@@ -427,12 +492,15 @@
             def _():
                 c_down(s).start()
 
-        put_rim(0)
         for c in range(0, tc, CHUNK):
             g_ref[c : c + CHUNK, 0:LANES] = one_hot(iota((CHUNK, LANES), 0) + c == row_idx)
             g_ref[c : c + CHUNK, LANES:] = one_hot(iota((CHUNK, LANES), 0) + c == edge_cols)
+        load_f.wait()
+        pl.semaphore_wait(barrier, expect)
         put_samples(0, gather(0, tc, (0, 2 * LANES)))
-        send_y[STEPS] = gather(2 * tc, tc, (LANES, 2 * LANES))
+        put_rim(0)
+        flows = gather(2 * tc, tc, (LANES, 2 * LANES))
+        send_y[1, STEPS] = jnp.where(left, pltpu.roll(flows[:half], HALF, 1), flows[half:])
 
         @pl.when(has_next_y)
         def _():
@@ -440,11 +508,11 @@
 
         for c in range(0, tc, CHUNK):
             at = iota((LANES, CHUNK), 1) + c
-            s_ref[0:LANES, c : c + CHUNK] = one_hot(at == col_ref[...])
+            s_ref[0:LANES, c : c + CHUNK] = one_hot(at == col_idx)
             s_ref[LANES:, c : c + CHUNK] = one_hot(at == first_spots)
             y_ref[:, c : c + CHUNK] = one_hot(at == last_spots)
-        mm_ref[0:LANES, 0:LANES] = one_hot(col_ref[...] == row_idx)
-        mm_ref[0:LANES, LANES:] = one_hot(col_ref[...] == edge_cols)
+        mm_ref[0:LANES, 0:LANES] = one_hot(col_idx == row_idx)
+        mm_ref[0:LANES, LANES:] = one_hot(col_idx == edge_cols)
         mm_ref[LANES:, 0:LANES] = one_hot(first_spots == row_idx)
         mm_ref[LANES:, LANES:] = one_hot(first_spots == edge_cols)
 
@@ -452,7 +520,7 @@
         def _():
             c_down(STEPS).wait_recv()
 
-        be_ref[...] = jnp.where(lane < rows, pltpu.roll(recv_yd[STEPS], HALF, 1), 0.0)
+        be_ref[...] = jnp.where(lane < rows, unfold(recv_yd[STEPS]), 0.0)
 
         place = iota((1, tc), 1)
         in_y = place % CY
@@ -496,12 +564,12 @@
             def _():
                 c_down(s).wait_recv()
 
-            lhs = split3(recv_yu[s])
+            lhs = split3(unfold(recv_yu[s]))
             for c in range(0, tc, CHUNK):
                 o_ref[:, 2 * tc + c : 2 * tc + c + CHUNK] -= FLUID_B * join3(
                     dot(lhs, y_ref[:, c : c + CHUNK])
                 )
-            behind = be_ref[...] - FLUID_B * (send_y[s] - pltpu.roll(recv_yd[s], HALF, 1))
+            behind = be_ref[...] - FLUID_B * (own_y[...] - unfold(recv_yd[s]))
             behind = jnp.where(jnp.logical_and(lane < rows, has_prev_y), behind, 0.0)
             be_ref[...] = behind
 
@@ -587,32 +655,22 @@
 def local(n_xy, n_guide, fields, rod_coeffs, rod_mask, pair_counts, fluid_slots, rod_slots, rod_sides):
     levels, width = fields.shape[1:]
     rc, tc = width // 9, width // 4
-    tile = lax.axis_index("xy")
-    is_solid = lax.axis_index("grp") == 0
-    slots = fluid_slots.shape[2]
-    offsets = jnp.array([0, 1, TILES_Y, TILES_Y + 1], dtype=jnp.int32)
-    owner_ids = jnp.arange(n_xy, dtype=jnp.int32)[:, None]
-    owners = jnp.where(is_solid, tile, (tile - offsets) % n_xy)
-    counts = jnp.sum(jnp.where(owner_ids == owners[None, :], pair_counts, 0), axis=0)
-    valid = (jnp.arange(slots, dtype=jnp.int32)[None, :] < counts[:, None]).reshape(-1)
-    sides = rod_sides[0].reshape(-1)
-    cols = jnp.where(
-        is_solid, sides // 2 * rc + rod_slots[0].reshape(-1), fluid_slots[0].reshape(-1)
-    )
-    facing = 2 * (sides % 2) - 1
-    row = jnp.stack([cols, facing])
-    col = jnp.where(valid, cols, -1).reshape(-1, 1)
     n_feet = 4 if n_xy > TILES_Y else 2
     n_x = 2 if n_xy > TILES_Y else 1
     x_steps = STEPS if n_xy > TILES_Y else 1
     rim = max(2 * rc, tc)
     vmem = pl.BlockSpec(memory_space=pltpu.VMEM)
+    smem = pl.BlockSpec(memory_space=pltpu.SMEM)
+    hbm = pl.BlockSpec(memory_space=pl.ANY)
     out = pl.pallas_call(
         functools.partial(kernel, n_xy, n_guide),
-        out_shape=jax.ShapeDtypeStruct((levels, width), F32),
-        in_specs=[vmem] * 5,
+        out_shape=pltpu.VMEM((levels, width), F32),
+        in_specs=[hbm, hbm, hbm, smem, vmem, vmem, vmem],
         out_specs=vmem,
         scratch_shapes=[
+            pltpu.VMEM((3, levels, rc), F32),
+            pltpu.VMEM((levels, rc), jnp.int32),
+            pltpu.SemaphoreType.DMA((3,)),
             pltpu.VMEM((tc, 2 * LANES), BF16),
             pltpu.VMEM((2 * LANES, tc), BF16),
             pltpu.VMEM((LANES, tc), BF16),
@@ -621,11 +679,12 @@
             pltpu.VMEM((levels, rc), F32),
             pltpu.VMEM((levels, LANES), F32),
             pltpu.VMEM((levels, 2 * LANES), F32),
-            pltpu.VMEM((STEPS, levels, LANES), F32),
-            pltpu.VMEM((STEPS, n_feet, levels, LANES), F32),
-            pltpu.VMEM((STEPS + 1, levels, LANES), F32),
-            pltpu.VMEM((STEPS + 1, levels, LANES), F32),
-            pltpu.VMEM((STEPS + 1, levels, LANES), F32),
+            pltpu.VMEM((STEPS, n_feet, 8, LANES), F32),
+            pltpu.VMEM((STEPS, n_feet, 8, LANES), F32),
+            pltpu.VMEM((levels, LANES), F32),
+            pltpu.VMEM((2, STEPS + 1, levels // 2, LANES), F32),
+            pltpu.VMEM((STEPS + 1, levels // 2, LANES), F32),
+            pltpu.VMEM((STEPS + 1, levels // 2, LANES), F32),
             pltpu.VMEM((4, STEPS, 1, rim), F32),
             pltpu.VMEM((4, STEPS, 1, rim), F32),
             pltpu.VMEM((n_x, x_steps, levels, LANES), F32),
@@ -634,7 +693,7 @@
             pltpu.SemaphoreType.DMA((n_feet + 8, STEPS + 1)),
         ],
         compiler_params=pltpu.CompilerParams(collective_id=0, has_side_effects=True),
-    )(fields[0], rod_coeffs, rod_mask, row, col)
+    )(fields[0], rod_coeffs, rod_mask, pair_counts, fluid_slots, rod_slots, rod_sides)
     return out[None]
 
 

time: 45 us -> 34.2 us (0.76)
  local copies, waits for them, and re-layouts: 7.13 us -> 1.02 us
  other arithmetic: 2.72 us -> 0 us
  Pallas kernels: 34.7 us -> 33 us
    another operation x6 -> x0, local copies, waits for them, and re-layouts: 4.65 us -> none  [the longest x2 1.55 us: local(): rod_slots[0].reshape(-1)]
    pallas_call x1, Pallas kernels: 34.7 us -> 33 us  [local(): pl.pallas_call(functools.partial(kernel, n_xy, n_guide), out_shape=pltpu....]
    select_n x3 -> x0, other arithmetic: 1.37 us -> none  [the longest x1 0.69 us: local(): col = jnp.where(valid, cols, -1).reshape(-1, 1)]
    unnamed x1, local copies, waits for them, and re-layouts: 2.36 us -> 1.02 us
    reduce_sum x1 -> x0, other arithmetic: 0.7 us -> none  [local(): jnp.sum(jnp.where(owner_ids == owners[None, :], pair_counts, 0), axis=0)]
    another operation x1 -> x0, other arithmetic: 0.58 us -> none  [local(): row = jnp.stack([cols, facing])]
where the time goes in v1:
time: 34.2 us; the launch traced here: 34 us
  Pallas kernels  33 us (96%)
  local copies, waits for them, and re-layouts  1.02 us (3%)
    pallas_call x1, Pallas kernels, local(): pl.pallas_call(functools.partial(kernel, n_xy, n_guide), out_shape=pltpu....  33 us
    unnamed x1, local copies, waits for them, and re-layouts  1.02 us

profile of v1, /device:TPU:1, one launch (start us, length us, event | category | flops | bytes accessed | tf_op | source)
XLA Modules:
  0.0 34.0 jit_solution(13378833080291305654)
XLA Ops:
  0.0 33.0 %shard_map.73 = f32[32,9216]{1,0:T(8,128)S(1)} custom-call(f32[32,9216]{1,0:T(8,128)} %bitcast.3, f32[3,32,1024]{2,1,0:T(8,128)} %c_hbm.1, s32[32,1024]{1,0:T(8,128)} %m_hbm.1, s32[4,4]{1,0:T(4,128)} %counts_ref.1, s32[1,4,32]{2,1,0:T(4,128)} %fluid_ref.1, s32[1,4,32]{2,1,0:T(4,128)} %rod_ref.1, s32[1,4,32]{2,1,0:T(4,128)} %sides_ref.1), custom_call_target="tpu_custom_call" | custom-call | tf_op jit(solution)/shard_map/pallas_call | solution.py:665
  33.0 1.0 %copy.9 = f32[1,32,9216]{2,1,0:T(8,128)} copy(f32[1,32,9216]{2,1,0:T(8,128)S(1)} %bitcast.2) | data formatting | bytes 2359296

commit v2 on v1

--- a/solution.py
+++ b/solution.py
@@ -304,15 +304,18 @@
         mm_ref[0:LANES, 0:LANES] = one_hot(col_idx == row_idx)
         load_f.wait()
 
-        def put_a(s):
+        def put_under(s):
             top = levels - 1
             send_rim[0, s, :, 0 : 2 * rc] = o_ref[top : top + 1, 7 * rc : 9 * rc]
+            c_rim(0, s, 2 * rc).start()
+
+        def put_over(s):
             send_rim[1, s, :, 0:rc] = o_ref[0:1, 5 * rc : 6 * rc]
-            c_rim(0, s, 2 * rc).start()
             c_rim(1, s, rc).start()
 
         pl.semaphore_wait(barrier, expect)
-        put_a(0)
+        put_over(0)
+        put_under(0)
         load_c.wait()
         load_m.wait()
         for r0 in range(0, levels, 8):
@@ -347,9 +350,11 @@
             o_ref[r0 : r0 + 8, member * rc : (member + 1) * rc] = v
 
         def step(s, carry):
-            c_rim(0, s, 2 * rc).wait_recv()
-            c_rim(1, s, rc).wait_recv()
-            for r0 in range(0, levels, 8):
+            for r0 in [*range(8, levels, 8), 0]:
+                if r0 == levels - 8:
+                    c_rim(1, s, rc).wait_recv()
+                if r0 == 0:
+                    c_rim(0, s, 2 * rc).wait_recv()
                 buo = c_ref[2, r0 : r0 + 8, :]
                 xy_ = comp(o_ref, 6, rc, r0)
                 xz = comp(o_ref, 7, rc, r0)
@@ -375,8 +380,9 @@
                     r0,
                     comp(o_ref, 2, rc, r0) + buo * (back_x(xz) + back_y(yz) + (zz_up - zz)),
                 )
-            send_rim[2, s, :, 0:rc] = o_ref[levels - 1 : levels, 2 * rc : 3 * rc]
-            c_rim(2, s, rc).start()
+                if r0 == levels - 8:
+                    send_rim[2, s, :, 0:rc] = o_ref[levels - 1 : levels, 2 * rc : 3 * rc]
+                    c_rim(2, s, rc).start()
             base = gather(0, 2 * rc, (0, LANES))
             each_foot(True, lambda o: c_foot(o, s, True).wait_recv())
             lhs = split3(incoming(s) * (-facing))
@@ -390,9 +396,11 @@
                 o_ref[:, c : c + CHUNK] += c_ref[2, :, c % rc : c % rc + CHUNK] * push
             send_rim[3, s, :, 0 : 2 * rc] = o_ref[0:1, 0 : 2 * rc]
             c_rim(3, s, 2 * rc).start()
-            c_rim(2, s, rc).wait_recv()
-            c_rim(3, s, 2 * rc).wait_recv()
-            for r0 in range(0, levels, 8):
+            for r0 in [*range(8, levels - 8, 8), 0, levels - 8]:
+                if r0 == 0:
+                    c_rim(2, s, rc).wait_recv()
+                if r0 == levels - 8:
+                    c_rim(3, s, 2 * rc).wait_recv()
                 sx = comp(o_ref, 0, rc, r0)
                 sy = comp(o_ref, 1, rc, r0)
                 sz = comp(o_ref, 2, rc, r0)
@@ -411,10 +419,15 @@
                 sy_up = upper(1, rc, r0, recv_rim[3, s, :, rc : 2 * rc])
                 store(7, r0, comp(o_ref, 7, rc, r0) + shear * (sx_up - sx + fore_x(sz)))
                 store(8, r0, comp(o_ref, 8, rc, r0) + shear * (sy_up - sy + fore_y(sz)))
+                if r0 == 0:
+
+                    @pl.when(s < STEPS - 1)
+                    def _():
+                        put_over(s + 1)
 
             @pl.when(s < STEPS - 1)
             def _():
-                put_a(s + 1)
+                put_under(s + 1)
 
             return carry
 
@@ -529,14 +542,9 @@
             o_ref[r0 : r0 + 8, member * tc : (member + 1) * tc] = v
 
         def step(s, carry):
-            c_rim(1, s, tc).wait_recv()
-            if tiles_x > 1:
-
-                @pl.when(has_next_x)
-                def _():
-                    c_x(0, s).wait_recv()
-
             for r0 in range(0, levels, 8):
+                if r0 == levels - 8:
+                    c_rim(1, s, tc).wait_recv()
                 p = comp(o_ref, 0, tc, r0)
                 next_x = jnp.where(place < tc - CY, pltpu.roll(p, tc - CY, 1), 0.0)
                 store(1, r0, comp(o_ref, 1, tc, r0) - FLUID_B * (next_x - p))
@@ -547,6 +555,11 @@
             send_rim[2, s, :, 0:tc] = o_ref[levels - 1 : levels, 3 * tc : 4 * tc]
             c_rim(2, s, tc).start()
             if tiles_x > 1:
+
+                @pl.when(has_next_x)
+                def _():
+                    c_x(0, s).wait_recv()
+
                 ahead = pltpu.roll(recv_x[0, s], LANES - CY, 1)
                 tail = slice(2 * tc - LANES, 2 * tc)
                 o_ref[:, tail] -= jnp.where(lane >= LANES - CY, FLUID_B * ahead, 0.0)
@@ -573,8 +586,9 @@
             behind = jnp.where(jnp.logical_and(lane < rows, has_prev_y), behind, 0.0)
             be_ref[...] = behind
 
-            c_rim(2, s, tc).wait_recv()
-            for r0 in range(0, levels, 8):
+            for r0 in [*range(8, levels, 8), 0]:
+                if r0 == 0:
+                    c_rim(2, s, tc).wait_recv()
                 fx = comp(o_ref, 1, tc, r0)
                 fy = comp(o_ref, 2, tc, r0)
                 fz = comp(o_ref, 3, tc, r0)

time: 34.2 us -> 34 us (level)
  no operation moved by 1% of the time
where the time goes in v2:
time: 34 us; the launch traced here: 33.9 us
  Pallas kernels  32.8 us (96%)
  local copies, waits for them, and re-layouts  1.02 us (3%)
    pallas_call x1, Pallas kernels, local(): pl.pallas_call(functools.partial(kernel, n_xy, n_guide), out_shape=pltpu....  32.8 us
    unnamed x1, local copies, waits for them, and re-layouts  1.02 us

profile of v2, /device:TPU:1, one launch (start us, length us, event | category | flops | bytes accessed | tf_op | source)
XLA Modules:
  0.0 33.9 jit_solution(35166930178874276)
XLA Ops:
  0.0 32.8 %shard_map.73 = f32[32,9216]{1,0:T(8,128)S(1)} custom-call(f32[32,9216]{1,0:T(8,128)} %bitcast.3, f32[3,32,1024]{2,1,0:T(8,128)} %c_hbm.1, s32[32,1024]{1,0:T(8,128)} %m_hbm.1, s32[4,4]{1,0:T(4,128)} %counts_ref.1, s32[1,4,32]{2,1,0:T(4,128)} %fluid_ref.1, s32[1,4,32]{2,1,0:T(4,128)} %rod_ref.1, s32[1,4,32]{2,1,0:T(4,128)} %sides_ref.1), custom_call_target="tpu_custom_call" | custom-call | tf_op jit(solution)/shard_map/pallas_call | solution.py:679
  32.8 1.0 %copy.9 = f32[1,32,9216]{2,1,0:T(8,128)} copy(f32[1,32,9216]{2,1,0:T(8,128)S(1)} %bitcast.2) | data formatting | bytes 2359296

commit v3 on v2

--- a/solution.py
+++ b/solution.py
@@ -276,7 +276,7 @@
                 moved = pltpu.roll(recv_i[s, o], ((o - b) * slots) % LANES, 1)
                 block = jnp.where(lane8 >= o * slots, moved, block)
             blocks.append(block)
-        return jnp.where(lane < nf * slots, jnp.concatenate(blocks, axis=0), 0.0)
+        return jnp.concatenate(blocks, axis=0)
 
     def each_foot(solid, act):
         for o in range(nf):
@@ -284,6 +284,14 @@
             @pl.when(foot_has(o, solid))
             def _():
                 act(o)
+
+    def send_feet(s, samples, solid):
+        for o in reversed(range(nf)):
+            send_i[s, o] = pack(samples, o)
+
+            @pl.when(foot_has(o, solid))
+            def _():
+                c_foot(o, s, solid).start()
 
     def no_feet(solid):
         for o in range(1, nf):
@@ -297,11 +305,15 @@
         no_feet(True)
         sides = sides_ref[0]
         row_idx, col_idx = slot_columns(sides // 2 * rc + rod_ref[0], lambda o: xy)
-        facing = 2.0 * as_row(as_column(sides % 2)) - 1.0
+        face_col = 2.0 * as_column(sides % 2) - 1.0
+        facing = as_row(face_col)
         for c in range(0, 2 * rc, CHUNK):
             g_ref[c : c + CHUNK, 0:LANES] = one_hot(iota((CHUNK, LANES), 0) + c == row_idx)
-            s_ref[0:LANES, c : c + CHUNK] = one_hot(iota((LANES, CHUNK), 1) + c == col_idx)
-        mm_ref[0:LANES, 0:LANES] = one_hot(col_idx == row_idx)
+            at = iota((LANES, CHUNK), 1) + c == col_idx
+            s_ref[0:LANES, c : c + CHUNK] = jnp.where(at, -face_col, 0.0).astype(BF16)
+        mm_ref[0:LANES, 0:LANES] = jnp.where(
+            col_idx == row_idx, -face_col * facing, 0.0
+        ).astype(BF16)
         load_f.wait()
 
         def put_under(s):
@@ -383,14 +395,11 @@
                 if r0 == levels - 8:
                     send_rim[2, s, :, 0:rc] = o_ref[levels - 1 : levels, 2 * rc : 3 * rc]
                     c_rim(2, s, rc).start()
-            base = gather(0, 2 * rc, (0, LANES))
+            base = gather(0, 2 * rc, (0, LANES)) * facing
             each_foot(True, lambda o: c_foot(o, s, True).wait_recv())
-            lhs = split3(incoming(s) * (-facing))
+            lhs = split3(incoming(s))
             normal = base + be_ref[...] * join3(dot(lhs, mm_ref[0:LANES, 0:LANES]))
-            normal = normal * facing
-            for o in range(nf):
-                send_i[s, o] = pack(normal, o)
-            each_foot(True, lambda o: c_foot(o, s, True).start())
+            send_feet(s, normal, True)
             for c in range(0, 2 * rc, CHUNK):
                 push = join3(dot(lhs, s_ref[0:LANES, c : c + CHUNK]))
                 o_ref[:, c : c + CHUNK] += c_ref[2, :, c % rc : c % rc + CHUNK] * push
@@ -487,12 +496,7 @@
                 def _():
                     c_x(0, s).start()
 
-        def put_samples(s, both):
-            samples = both[:, :LANES]
-            for o in range(nf):
-                send_i[s, o] = pack(samples, o)
-            each_foot(False, lambda o: c_foot(o, s, False).start())
-            edges = both[:, LANES:]
+        def put_edges(s, edges):
             own_y[...] = edges
             send_y[0, s] = jnp.where(left, edges[:half], pltpu.roll(edges[half:], HALF, 1))
             send_y[1, s] = jnp.where(left, pltpu.roll(edges[:half], HALF, 1), edges[half:])
@@ -510,7 +514,9 @@
             g_ref[c : c + CHUNK, LANES:] = one_hot(iota((CHUNK, LANES), 0) + c == edge_cols)
         load_f.wait()
         pl.semaphore_wait(barrier, expect)
-        put_samples(0, gather(0, tc, (0, 2 * LANES)))
+        both = gather(0, tc, (0, 2 * LANES))
+        send_feet(0, both[:, :LANES], False)
+        put_edges(0, both[:, LANES:])
         put_rim(0)
         flows = gather(2 * tc, tc, (LANES, 2 * LANES))
         send_y[1, STEPS] = jnp.where(left, pltpu.roll(flows[:half], HALF, 1), flows[half:])
@@ -612,17 +618,24 @@
 
             @pl.when(s < STEPS - 1)
             def _():
-                ebase_ref[...] = gather(0, tc, (0, 2 * LANES))
+                ebase_ref[...] = gather(0, tc, (0, 2 * LANES)) + FLUID_A * join3(
+                    dot(split3(behind), mm_ref[LANES:, :])
+                )
 
             each_foot(False, lambda o: c_foot(o, s, False).wait_recv())
-            lhs = split3(jnp.concatenate([incoming(s), behind], axis=1))
+            arrived = split3(incoming(s))
 
             @pl.when(s < STEPS - 1)
             def _():
-                put_samples(
-                    s + 1, ebase_ref[...] + FLUID_A * join3(dot(lhs, mm_ref[...]))
-                )
-
+                for part in (slice(0, LANES), slice(LANES, 2 * LANES)):
+                    pushed = join3(dot(arrived, mm_ref[0:LANES, part]))
+                    samples = ebase_ref[:, part] + FLUID_A * pushed
+                    if part.start == 0:
+                        send_feet(s + 1, samples, False)
+                    else:
+                        put_edges(s + 1, samples)
+
+            lhs = jnp.concatenate([arrived, split3(behind)], axis=1)
             for c in range(0, tc, CHUNK):
                 o_ref[:, c : c + CHUNK] += FLUID_A * join3(dot(lhs, s_ref[:, c : c + CHUNK]))
 

time: 34 us -> 33.9 us (level)
  no operation moved by 1% of the time
where the time goes in v3:
time: 33.9 us; the launch traced here: 33.7 us
  Pallas kernels  32.7 us (96%)
  local copies, waits for them, and re-layouts  1.02 us (3%)
    pallas_call x1, Pallas kernels, local(): pl.pallas_call(functools.partial(kernel, n_xy, n_guide), out_shape=pltpu....  32.7 us
    unnamed x1, local copies, waits for them, and re-layouts  1.02 us

profile of v3, /device:TPU:1, one launch (start us, length us, event | category | flops | bytes accessed | tf_op | source)
XLA Modules:
  0.0 33.7 jit_solution(11382568200911070896)
XLA Ops:
  0.0 32.7 %shard_map.73 = f32[32,9216]{1,0:T(8,128)S(1)} custom-call(f32[32,9216]{1,0:T(8,128)} %bitcast.3, f32[3,32,1024]{2,1,0:T(8,128)} %c_hbm.1, s32[32,1024]{1,0:T(8,128)} %m_hbm.1, s32[4,4]{1,0:T(4,128)} %counts_ref.1, s32[1,4,32]{2,1,0:T(4,128)} %fluid_ref.1, s32[1,4,32]{2,1,0:T(4,128)} %rod_ref.1, s32[1,4,32]{2,1,0:T(4,128)} %sides_ref.1), custom_call_target="tpu_custom_call" | custom-call | tf_op jit(solution)/shard_map/pallas_call | solution.py:692
  32.7 1.0 %copy.9 = f32[1,32,9216]{2,1,0:T(8,128)} copy(f32[1,32,9216]{2,1,0:T(8,128)S(1)} %bitcast.2) | data formatting | bytes 2359296
